TPU v7x, 256 devices: a whole 4x4x8 slice. The times are simulated.
256 devices in a mesh: ctx: 32 (over x_lo, z, core), exp: 8 (over x_hi, y).
Axes of the slice: x: 4 (x_hi: 2, x_lo: 2; x = x_hi * 2 + x_lo), y: 4, z: 8, core: 2. Of those that a mesh axis runs over, the one named last changes fastest.
Arguments:
- queries: bfloat16 [8192, 8192], P('ctx', 'exp'), may hold values from -8 to 8
- keys: bfloat16 [8192, 512], P('ctx'), may hold values from -4 to 4
- values: bfloat16 [8192, 512], P('ctx'), may hold values from -6 to 6
- w_out: bfloat16 [8192, 4096], P('exp'), may hold values from -0.5 to 0.5
- residual: bfloat16 [8192, 4096], P(('ctx', 'exp')), may hold values from -1.5 to 1.5
- norm_gain: bfloat16 [4096], replicated, may hold values from 0.099609375 to 1.8984375
- expert_ids: int32 [8192, 2], P(('ctx', 'exp')), may hold values from 0 to 7, all different within a row; in each aligned block of 32 rows (0 to 31, 32 to 63, ...) at most 16 rows name the same one
- gate_weights: float32 [8192, 2], P(('ctx', 'exp')), may hold values from 0.2 to 1
- w_gate: bfloat16 [8, 4096, 768], P('exp', 'ctx'), may hold values from -0.09375 to 0.09375
- w_up: bfloat16 [8, 4096, 768], P('exp', 'ctx'), may hold values from -0.09375 to 0.09375
- w_down: bfloat16 [8, 768, 4096], P('exp', None, 'ctx'), may hold values from -0.21875 to 0.21875
Outputs:
- layer_out: bfloat16 [8192, 4096], P(('ctx', 'exp'))
Inputs may be any that keep to these rules, and one draw needn't show every extreme that they name: `expert_ids`: each row names 2 different experts; within each aligned block of 32 rows (the rows of one device) no expert is named by more than 16 rows.
All inputs are finite; a program needn't handle non-finite values.
Results may differ from a plain program's by a relative error of at most 0.025.
Values may be sent and summed in bfloat16 or wider, within the bound.
A program may use at most 128 MiB of HBM per device.

v0:
```python
import math
import jax
import jax.numpy as jnp
from jax import lax
from jax.sharding import PartitionSpec as P

D = 4096
HQ = 64
KVH = 4
HD = 128


def body(
    queries,
    keys,
    values,
    w_out,
    residual,
    norm_gain,
    expert_ids,
    gate_weights,
    w_gate,
    w_up,
    w_down,
):
    tok_rows = queries.shape[0]
    half_rows = tok_rows // 2
    exp_count = lax.axis_size("exp")
    heads_here = HQ // exp_count
    group = HQ // KVH
    kv_here = max(1, heads_here // group)
    heads_per_kv = heads_here // kv_here
    exp_index = lax.axis_index("exp")
    ctx_index = lax.axis_index("ctx")
    kv_first = exp_index * heads_here // group
    key_cols = lax.dynamic_slice_in_dim(keys, kv_first * HD, kv_here * HD, 1)
    value_cols = lax.dynamic_slice_in_dim(values, kv_first * HD, kv_here * HD, 1)
    scale = 1.0 / math.sqrt(HD)
    first_rows = queries[:half_rows]
    second_rows = queries[half_rows:]
    first_start = ctx_index * tok_rows
    second_start = ctx_index * tok_rows + half_rows
    query_sets = (
        first_rows.reshape(half_rows, kv_here, heads_per_kv, HD),
        second_rows.reshape(half_rows, kv_here, heads_per_kv, HD),
    )
    query_positions = (
        first_start + jnp.arange(half_rows, dtype=jnp.int32),
        second_start + jnp.arange(half_rows, dtype=jnp.int32),
    )
    last_positions = (first_start + half_rows - 1, second_start + half_rows - 1)

    def block_update(carry, query_four, query_pos, key_block, value_block, key_start):
        run_max, run_sum, run_acc = carry
        width = key_block.shape[0]
        key_three = key_block.reshape(width, kv_here, HD)
        value_three = value_block.reshape(width, kv_here, HD)
        scores = (
            jnp.einsum("tghd,kgd->ghtk", query_four, key_three, preferred_element_type=jnp.float32)
            * scale
        )
        key_pos = key_start + jnp.arange(width, dtype=jnp.int32)
        allowed = key_pos[None, :] <= query_pos[:, None]
        scores = jnp.where(allowed, scores, -1e30)
        new_max = jnp.maximum(run_max, jnp.max(scores, axis=-1))
        probs = jnp.where(allowed, jnp.exp(scores - new_max[..., None]), 0.0)
        factor = jnp.exp(run_max - new_max)
        run_sum = run_sum * factor + jnp.sum(probs, axis=-1)
        weighted = jnp.einsum(
            "ghtk,kgd->ghtd",
            probs.astype(jnp.bfloat16),
            value_three,
            preferred_element_type=jnp.float32,
        )
        run_acc = run_acc * factor[..., None] + weighted
        return (new_max, run_sum, run_acc)

    start_max = jnp.full((kv_here, heads_per_kv, half_rows), -1e30, jnp.float32)
    start_sum = jnp.zeros((kv_here, heads_per_kv, half_rows), jnp.float32)
    start_acc = jnp.zeros((kv_here, heads_per_kv, half_rows, HD), jnp.float32)
    start_state = (start_max, start_sum, start_acc)
    key_piece = lax.all_gather(key_cols, "ctx", axis=0, tiled=True)
    value_piece = lax.all_gather(value_cols, "ctx", axis=0, tiled=True)
    count = key_piece.shape[0]
    width = 512

    def one_block(index, inner):
        key_start = index * width
        key_block = lax.dynamic_slice_in_dim(key_piece, key_start, width, 0)
        value_block = lax.dynamic_slice_in_dim(value_piece, key_start, width, 0)
        updated = []
        for which in range(2):
            query_four = query_sets[which]
            query_pos = query_positions[which]
            updated.append(
                lax.cond(
                    key_start > last_positions[which],
                    lambda state: state,
                    lambda state: block_update(
                        state, query_four, query_pos, key_block, value_block, key_start
                    ),
                    inner[which],
                )
            )
        return (updated[0], updated[1])

    states = lax.fori_loop(0, count // width, one_block, (start_state, start_state))
    halves = []
    for which in range(2):
        run_max, run_sum, run_acc = states[which]
        halves.append(
            jnp.transpose(run_acc / run_sum[..., None], (2, 0, 1, 3))
            .reshape(half_rows, heads_here * HD)
            .astype(jnp.bfloat16)
        )
    attn_second = halves[1]
    attn = jnp.concatenate([halves[0], attn_second], axis=0)
    projected = lax.psum_scatter(
        jnp.dot(attn, w_out, preferred_element_type=jnp.float32).astype(jnp.bfloat16),
        "exp",
        scatter_dimension=0,
        tiled=True,
    ).astype(jnp.float32)
    hidden_state = (residual.astype(jnp.float32) + projected).astype(jnp.bfloat16)
    state_f = hidden_state.astype(jnp.float32)
    inv_rms = 1.0 / jnp.sqrt(jnp.mean(state_f * state_f, axis=1, keepdims=True) + 1e-06)
    normed = (state_f * inv_rms * norm_gain.astype(jnp.float32)[None, :]).astype(jnp.bfloat16)
    rows_here = expert_ids.shape[0]
    top_count = expert_ids.shape[1]
    experts_all = w_gate.shape[0] * exp_count
    capacity = min(rows_here, 2 * rows_here * top_count // experts_all)
    flat_ids = expert_ids.reshape(-1)
    onehot = (flat_ids[:, None] == jnp.arange(experts_all, dtype=jnp.int32)[None, :]).astype(
        jnp.int32
    )
    earlier = jnp.cumsum(onehot, axis=0) - onehot
    slot_index = jnp.sum(earlier * onehot, axis=1)
    target = flat_ids * capacity + slot_index
    picks = target[:, None] == jnp.arange(experts_all * capacity, dtype=jnp.int32)[None, :]
    dispatch_table = jnp.any(
        picks.reshape(rows_here, top_count, experts_all * capacity), axis=1
    ).astype(jnp.bfloat16)
    outgoing = jnp.einsum(
        "rs,rd->sd", dispatch_table, normed, preferred_element_type=jnp.float32
    ).astype(jnp.bfloat16)
    arrived = lax.all_to_all(
        outgoing.reshape(experts_all, capacity, D), "exp", split_axis=0, concat_axis=0, tiled=True
    )
    slot_rows = arrived.reshape(experts_all * capacity, D)
    gate_local = w_gate[0]
    up_local = w_up[0]
    gate_pre = jnp.dot(
        slot_rows,
        lax.all_gather(gate_local, "ctx", axis=0, tiled=True),
        preferred_element_type=jnp.float32,
    )
    up_pre = jnp.dot(
        slot_rows,
        lax.all_gather(up_local, "ctx", axis=0, tiled=True),
        preferred_element_type=jnp.float32,
    )
    expert_hidden = (jax.nn.silu(gate_pre) * up_pre).astype(jnp.bfloat16)
    down_local = w_down[0]
    expert_result = jnp.dot(
        expert_hidden,
        lax.all_gather(down_local, "ctx", axis=1, tiled=True),
        preferred_element_type=jnp.float32,
    ).astype(jnp.bfloat16)
    returned = lax.all_to_all(
        expert_result.reshape(experts_all, capacity, D),
        "exp",
        split_axis=0,
        concat_axis=0,
        tiled=True,
    )
    returned_flat = returned.reshape(experts_all * capacity, D)
    picked = jnp.dot(picks.astype(jnp.bfloat16), returned_flat, preferred_element_type=jnp.float32)
    weighted = gate_weights[:, :, None] * picked.reshape(rows_here, top_count, D)
    return (state_f + jnp.sum(weighted, axis=1)).astype(jnp.bfloat16)


def solution(mesh):
    placed = (
        P("ctx", "exp"),
        P("ctx", None),
        P("ctx", None),
        P("exp", None),
        P(("ctx", "exp"), None),
        P(),
        P(("ctx", "exp"), None),
        P(("ctx", "exp"), None),
        P("exp", "ctx", None),
        P("exp", "ctx", None),
        P("exp", None, "ctx"),
    )
    return jax.shard_map(
        body, mesh=mesh, in_specs=placed, out_specs=P(("ctx", "exp"), None), check_vma=False
    )
```

profile of v0, /device:TPU:2, one launch (start us, length us, event | category | flops | bytes accessed | tf_op | source)
XLA Modules:
  0.0 573.4 jit_solution(10112256670926563452)
XLA Ops:
  8.2 1.5 constant_dynamic-slice_fusion.3
  9.7 1.1 fusion.83
  11.5 64.9 %all-gather.11.cloned.1.call-done = bf16[8192,128]{1,0:T(8,128)(2,1)} async-done(((bf16[256,128]{1,0:T(8,128)(2,1)}), bf16[8192,128]{1,0:T(8,128)(2,1)}) %all-gather.11.cloned.1.call-update) | async-done | bytes 2097168 | tf_op jit(solution)/shard_map/all_gather | solution.py:83
  76.4 66.3 %all-gather.9.cloned.1.call-done = bf16[8192,128]{1,0:T(8,128)(2,1)} async-done(((bf16[256,128]{1,0:T(8,128)(2,1)}), bf16[8192,128]{1,0:T(8,128)(2,1)}) %all-gather.9.cloned.1.call-update) | async-done | bytes 2097168 | tf_op jit(solution)/shard_map/all_gather | solution.py:82
  142.8 54.4 %while.24 = (s32[]{:T(128)}, f32[1,8,128]{2,1,0:T(8,128)S(1)}, f32[1,8,128]{2,1,0:T(8,128)S(1)}, f32[1,8,128,128]{3,2,1,0:T(8,128)S(1)}, f32[1,8,128]{2,1,0:T(8,...) while((s32[]{:T(128)}, f32[1,8,128]{2,1,0:T(8,128)S(1)}, ...), condition=%wide.region_9.10_spmd.clone, body=%wide.region_0.9_spmd.clone.sunk | while | flops 551165184 | bytes 16921084 | solution.py:107
  142.8 1.0 constant_dynamic-slice_fusion.5
  143.8 2.0 conditional.7
  145.9 2.0 conditional.6
  148.0 1.0 constant_dynamic-slice_fusion.5
  149.0 2.0 conditional.7
  151.1 2.0 conditional.6
  153.1 1.0 constant_dynamic-slice_fusion.5
  154.1 2.0 conditional.7
  156.2 2.0 conditional.6
  158.3 1.0 constant_dynamic-slice_fusion.5
  159.3 2.0 conditional.7
  161.4 2.0 conditional.6
  163.4 1.0 constant_dynamic-slice_fusion.5
  164.5 2.0 conditional.7
  166.5 2.0 conditional.6
  168.6 1.0 constant_dynamic-slice_fusion.5
  169.6 2.0 conditional.7
  171.7 2.0 conditional.6
  173.8 1.0 constant_dynamic-slice_fusion.5
  174.8 2.0 conditional.7
  176.8 2.0 conditional.6
  178.9 1.0 constant_dynamic-slice_fusion.5
  179.9 2.0 conditional.7
  182.0 2.0 conditional.6
  184.1 1.0 constant_dynamic-slice_fusion.5
  185.1 2.0 conditional.7
  187.1 2.0 conditional.6
  189.2 1.0 constant_dynamic-slice_fusion.5
  190.4 1.0 constant_dynamic-slice_fusion.5
  191.5 1.0 constant_dynamic-slice_fusion.5
  192.7 1.0 constant_dynamic-slice_fusion.5
  195.0 1.0 constant_dynamic-slice_fusion.5
  197.8 7.1 %convolution_convert_fusion = bf16[256,4096]{1,0:T(8,128)(2,1)} fusion(bf16[1024,4096]{1,0:T(8,128)(2,1)} %param.20, bf16[128,1024]{0,1:T(8,128)(2,1)S(1)} %bitcast.139, bf16[128,1024]{0,1:T(8,128)(2,1)S(1)} %bitcast.138), kind=kOutput, calls=%fused_computation.64 | convolution fusion | flops 2149580800 | bytes 11010048 | tf_op jit(solution)/shard_map/dot_general | solution.py:119
  207.5 101.7 %reduce-scatter.2.cloned.1.call-done = bf16[32,4096]{1,0:T(8,128)(2,1)} async-done(((bf16[256,4096]{1,0:T(8,128)(2,1)}), bf16[32,4096]{1,0:T(8,128)(2,1)}) %reduce-scatter.2.cloned.1.call-update) | async-done | bytes 262160 | tf_op jit(solution)/shard_map/reduce_scatter | solution.py:118
  309.2 1.1 fusion.60
  310.3 1.5 convolution_convert_fusion.1
  311.8 25.3 %all_to_all.10 = bf16[8,16,4096]{2,1,0:T(8,128)(2,1)S(1)} all-to-all(bf16[8,16,4096]{2,1,0:T(8,128)(2,1)S(1)} %bitcast.130), channel_id=1, replica_groups=mesh['ctx'=32,'exp'=8] {'exp'}, dimensions={0} | all-to-all | bytes 2097152 | tf_op jit(solution)/shard_map/all_to_all | solution.py:146
  337.1 43.7 %all-gather.13.cloned.1.call-done = bf16[1,4096,768]{2,1,0:T(8,128)(2,1)} async-done(((bf16[1,128,768]{2,1,0:T(8,128)(2,1)}), bf16[1,4096,768]{2,1,0:T(8,128)(2,1)}) %all-gather.13.cloned.1.call-update) | async-done | bytes 6291472 | tf_op jit(solution)/shard_map/all_gather | solution.py:154
  380.8 3.8 fusion.46
  384.6 67.9 %all-gather.15.cloned.1.call-done = bf16[1,4096,768]{2,1,0:T(8,128)(2,1)} async-done(((bf16[1,128,768]{2,1,0:T(8,128)(2,1)}), bf16[1,4096,768]{2,1,0:T(8,128)(2,1)}) %all-gather.15.cloned.1.call-update) | async-done | bytes 6291472 | tf_op jit(solution)/shard_map/all_gather | solution.py:159
  452.5 82.3 %all-gather.17.cloned.1.call-done = bf16[1,768,4096]{2,1,0:T(8,128)(2,1)} async-done(((bf16[1,768,128]{2,1,0:T(8,128)(2,1)}), bf16[1,768,4096]{2,1,0:T(8,128)(2,1)}) %all-gather.17.cloned.1.call-update) | async-done | bytes 6291472 | tf_op jit(solution)/shard_map/all_gather | solution.py:166
  534.7 7.1 %fusion.48 = bf16[128,4096]{1,0:T(8,128)(2,1)S(1)} fusion(bf16[1,768,4096]{2,1,0:T(8,128)(2,1)} %all-gather.17.cloned.1.call-done, bf16[128,4096]{1,0:T(8,128)(2,1)S(1)} %bitcast.128, bf16[1,4096,768]{2,1,0:T(8,128)(2,1)} %all-gather.15.cloned.1.call-done, f32[128,768]{1,0:T(8,128)S(1)} %fusion.46), kind=kOutput, calls=%fused_computation.65 | convolution fusion | flops 1611726848 | bytes 15073280 | tf_op jit(solution)/shard_map/dot_general | solution.py:164
  541.8 23.5 %all_to_all.11 = bf16[8,16,4096]{2,1,0:T(8,128)(2,1)S(1)} all-to-all(bf16[8,16,4096]{2,1,0:T(8,128)(2,1)S(1)} %bitcast.129), channel_id=1, replica_groups=mesh['ctx'=32,'exp'=8] {'exp'}, dimensions={0} | all-to-all | bytes 2097152 | tf_op jit(solution)/shard_map/all_to_all | solution.py:169
  (290 shorter events, 44.6 us)
Async XLA Ops:
  6.5 1.0 copy-start
  6.5 69.9 %all-gather.11.cloned.1.call-start = ((), (), s32[]{:S(2)}) async-start(), calls=%async_computation.4 | async-start | bytes 2162688 | tf_op jit(solution)/shard_map/all_gather | solution.py:83
  8.1 134.5 %all-gather.9.cloned.1.call-start = ((), (), s32[]{:S(2)}) async-start(), calls=%async_computation.3 | async-start | bytes 2162688 | tf_op jit(solution)/shard_map/all_gather | solution.py:82
  9.7 299.5 %reduce-scatter.2.cloned.1.call-start = ((), (), s32[]{:S(2)}) async-start(), calls=%async_computation.5 | async-start | bytes 2359296 | tf_op jit(solution)/shard_map/reduce_scatter | solution.py:118
  204.8 1.8 copy-start.4
  204.8 2.5 copy-start.3
  204.8 104.3 %copy-start.1 = (bf16[32,4096]{1,0:T(8,128)(2,1)S(1)}, bf16[32,4096]{1,0:T(8,128)(2,1)}, u32[]{:S(2)}) copy-start(bf16[32,4096]{1,0:T(8,128)(2,1)} %param.21) | copy-start | bytes 786436
  204.9 176.0 %all-gather.13.cloned.1.call-start = ((), (), s32[]{:S(2)}) async-start(), calls=%async_computation.6 | async-start | bytes 6488064 | tf_op jit(solution)/shard_map/all_gather | solution.py:154
  205.4 247.0 %all-gather.15.cloned.1.call-start = ((), (), s32[]{:S(2)}) async-start(), calls=%async_computation.7 | async-start | bytes 6488064 | tf_op jit(solution)/shard_map/all_gather | solution.py:159
  206.0 328.7 %all-gather.17.cloned.1.call-start = ((), (), s32[]{:S(2)}) async-start(), calls=%async_computation.8 | async-start | bytes 6488064 | tf_op jit(solution)/shard_map/all_gather | solution.py:166
  541.8 23.6 %copy-start.5 = (f32[32,2]{0,1:T(2,128)S(1)}, f32[32,2]{0,1:T(2,128)}, u32[]{:S(2)}) copy-start(f32[32,2]{0,1:T(2,128)} %param.24) | copy-start | bytes 772
  541.8 23.9 %copy-start.2 = (bf16[32,4096]{1,0:T(8,128)(2,1)S(1)}, bf16[32,4096]{1,0:T(8,128)(2,1)}, u32[]{:S(2)}) copy-start(bf16[32,4096]{1,0:T(8,128)(2,1)} %reduce-scatter.2.cloned.1.call-done) | copy-start | bytes 786436
Sparse Core Ops, SparseCore 0:
  9.2 67.1 all-gather.10
  78.3 64.3 all-gather.8
  205.0 104.1 reduce-scatter.1
  310.9 69.8 all-gather.12
  382.5 69.9 all-gather.14
  454.1 80.5 all-gather.16
where the time goes:
time: 574 us; the launch traced here: 573 us
  waiting for transfers between devices  428 us (75%)
  blocking collectives  48.9 us (9%)
  matrix products  42.9 us (7%)
  local copies, waits for them, and re-layouts  21.8 us (4%)
  other arithmetic  14.7 us (3%)
  between operations  13.7 us (2%)
    reduce_scatter x1, waiting for transfers between devices, body(): lax.psum_scatter(jnp.dot(attn, w_out, preferred_element_type=jnp.float32)...  102 us
    all_gather x1, waiting for transfers between devices, body(): lax.all_gather(down_local, 'ctx', axis=1, tiled=True)  82.3 us
    all_gather x1, waiting for transfers between devices, body(): lax.all_gather(up_local, 'ctx', axis=0, tiled=True)  67.9 us
    all_gather x1, waiting for transfers between devices, body(): key_piece = lax.all_gather(key_cols, 'ctx', axis=0, tiled=True)  66.3 us
    all_gather x1, waiting for transfers between devices, body(): value_piece = lax.all_gather(value_cols, 'ctx', axis=0, tiled=True)  64.9 us
    all_gather x1, waiting for transfers between devices, body(): lax.all_gather(gate_local, 'ctx', axis=0, tiled=True)  43.7 us
    all_to_all x1, blocking collectives, body(): lax.all_to_all(outgoing.reshape(experts_all, capacity, D), 'exp', split_a...  25.3 us
    all_to_all x1, blocking collectives, body(): lax.all_to_all(expert_result.reshape(experts_all, capacity, D), 'exp', sp...  23.5 us
  transfers between devices with their start and end apart: 6, of which 6 were waited for; matrix products, arithmetic and copies ran while one was open for 2% of the time, Pallas kernels for 0%

commit v1 on v0

--- a/solution.py
+++ b/solution.py
@@ -79,8 +79,11 @@
     start_sum = jnp.zeros((kv_here, heads_per_kv, half_rows), jnp.float32)
     start_acc = jnp.zeros((kv_here, heads_per_kv, half_rows, HD), jnp.float32)
     start_state = (start_max, start_sum, start_acc)
-    key_piece = lax.all_gather(key_cols, "ctx", axis=0, tiled=True)
-    value_piece = lax.all_gather(value_cols, "ctx", axis=0, tiled=True)
+    key_piece, value_piece = jnp.split(
+        lax.all_gather(jnp.concatenate([key_cols, value_cols], axis=1), "ctx", axis=0, tiled=True),
+        [key_cols.shape[1]],
+        axis=1,
+    )
     count = key_piece.shape[0]
     width = 512
 

time: 574 us -> 527 us (0.918)
  waiting for transfers between devices: 428 us -> 391 us
  blocking collectives: 48.9 us -> 23.5 us
  local copies, waits for them, and re-layouts: 21.8 us -> 31.6 us
    all_gather x2 -> x1, waiting for transfers between devices: 131 us -> 68.4 us  [body(): lax.all_gather(jnp.concatenate([key_cols, value_cols], axis=1), 'ctx', ax...]
    all_to_all x1 -> x0, blocking collectives: 25.3 us -> none  [body(): lax.all_to_all(outgoing.reshape(experts_all, capacity, D), 'exp', split_a...]
    all_gather x1, waiting for transfers between devices: 43.7 us -> 63.4 us  [body(): lax.all_gather(gate_local, 'ctx', axis=0, tiled=True)]
    cond x14 -> x50, local copies, waits for them, and re-layouts: 0.04 us -> 7.39 us
  transfers between devices with their start and end apart: 6 -> 6, of which waited for: 6 -> 5; matrix products, arithmetic and copies ran while one was open for 2% -> 2% of each run, Pallas kernels for 0% -> 0%
where the time goes in v1:
time: 527 us; the launch traced here: 526 us
  waiting for transfers between devices  391 us (74%)
  matrix products  43.8 us (8%)
  local copies, waits for them, and re-layouts  31.6 us (6%)
  blocking collectives  23.5 us (4%)
  other arithmetic  15.3 us (3%)
  between operations  13.3 us (3%)
    reduce_scatter x1, waiting for transfers between devices, body(): lax.psum_scatter(jnp.dot(attn, w_out, preferred_element_type=jnp.float32)...  107 us
    all_gather x1, waiting for transfers between devices, body(): lax.all_gather(down_local, 'ctx', axis=1, tiled=True)  82.3 us
    all_gather x1, waiting for transfers between devices, body(): lax.all_gather(jnp.concatenate([key_cols, value_cols], axis=1), 'ctx', ax...  68.4 us
    all_gather x1, waiting for transfers between devices, body(): lax.all_gather(up_local, 'ctx', axis=0, tiled=True)  68.2 us
    all_gather x1, waiting for transfers between devices, body(): lax.all_gather(gate_local, 'ctx', axis=0, tiled=True)  63.4 us
    all_to_all x1, blocking collectives, body(): lax.all_to_all(expert_result.reshape(experts_all, capacity, D), 'exp', sp...  23.5 us
    dot_general x18, matrix products, block_update(): jnp.einsum('ghtk,kgd->ghtd', probs.astype(jnp.bfloat16), value_three, pre...  15 us
    dynamic_slice x16, local copies, waits for them, and re-layouts, one_block(): value_block = lax.dynamic_slice_in_dim(value_piece, key_start, width, 0)  14.8 us
  transfers between devices with their start and end apart: 6, of which 5 were waited for; matrix products, arithmetic and copies ran while one was open for 2% of the time, Pallas kernels for 0%

profile of v1, /device:TPU:2, one launch (start us, length us, event | category | flops | bytes accessed | tf_op | source)
XLA Modules:
  0.0 526.0 jit_solution(14693672012487523443)
XLA Ops:
  8.2 1.1 fusion.84
  10.0 68.4 %all-gather.8.cloned.1.call-done = bf16[8192,256]{1,0:T(8,128)(2,1)} async-done(((bf16[256,256]{1,0:T(8,128)(2,1)}), bf16[8192,256]{1,0:T(8,128)(2,1)}) %all-gather.8.cloned.1.call-update) | async-done | bytes 4194320 | tf_op jit(solution)/shard_map/all_gather | solution.py:83
  78.4 3.8 fusion.83
  83.1 60.4 %while.24 = (s32[]{:T(128)}, f32[1,8,128]{2,1,0:T(8,128)S(1)}, f32[1,8,128]{2,1,0:T(8,128)S(1)}, f32[1,8,128,128]{3,2,1,0:T(8,128)S(1)}, f32[1,8,128]{2,1,0:T(8,...) while((s32[]{:T(128)}, f32[1,8,128]{2,1,0:T(8,128)S(1)}, ...), condition=%wide.region_9.10_spmd.clone, body=%wide.region_0.9_spmd.clone.sunk | while | flops 551165184 | bytes 21115444 | solution.py:110
  83.2 0.9 constant_dynamic-slice_fusion.5
  84.1 2.9 conditional.7
  87.0 2.0 conditional.6
  89.0 0.9 constant_dynamic-slice_fusion.5
  90.0 2.9 conditional.7
  92.8 2.0 conditional.6
  94.9 0.9 constant_dynamic-slice_fusion.5
  95.8 2.9 conditional.7
  98.7 2.0 conditional.6
  100.8 0.9 constant_dynamic-slice_fusion.5
  101.7 2.9 conditional.7
  104.6 2.0 conditional.6
  106.6 0.9 constant_dynamic-slice_fusion.5
  107.6 2.9 conditional.7
  110.4 2.0 conditional.6
  112.5 0.9 constant_dynamic-slice_fusion.5
  113.5 2.9 conditional.7
  116.3 2.0 conditional.6
  118.4 0.9 constant_dynamic-slice_fusion.5
  119.3 2.9 conditional.7
  122.2 2.0 conditional.6
  124.2 0.9 constant_dynamic-slice_fusion.5
  125.2 2.9 conditional.7
  128.1 2.0 conditional.6
  130.1 0.9 constant_dynamic-slice_fusion.5
  131.1 2.9 conditional.7
  133.9 2.0 conditional.6
  136.0 0.9 constant_dynamic-slice_fusion.5
  137.1 0.9 constant_dynamic-slice_fusion.5
  140.3 0.9 constant_dynamic-slice_fusion.5
  141.4 0.9 constant_dynamic-slice_fusion.5
  142.5 0.9 constant_dynamic-slice_fusion.5
  143.8 1.2 copy.50
  145.1 7.1 %convolution_convert_fusion = bf16[256,4096]{1,0:T(8,128)(2,1)} fusion(bf16[1024,4096]{1,0:T(8,128)(2,1)} %param.20, bf16[128,1024]{0,1:T(8,128)(2,1)S(1)} %bitcast.138, bf16[128,1024]{0,1:T(8,128)(2,1)S(1)} %bitcast.137), kind=kOutput, calls=%fused_computation.64 | convolution fusion | flops 2149580800 | bytes 11010048 | tf_op jit(solution)/shard_map/dot_general | solution.py:122
  155.0 107.0 %reduce-scatter.2.cloned.1.call-done = bf16[32,4096]{1,0:T(8,128)(2,1)} async-done(((bf16[256,4096]{1,0:T(8,128)(2,1)}), bf16[32,4096]{1,0:T(8,128)(2,1)}) %reduce-scatter.2.cloned.1.call-update) | async-done | bytes 262160 | tf_op jit(solution)/shard_map/reduce_scatter | solution.py:121
  262.0 1.1 fusion.60
  263.1 2.4 convolution_convert_fusion.1
  265.5 4.5 all-to-all-start
  270.1 63.4 %all-gather.10.cloned.1.call-done = bf16[1,4096,768]{2,1,0:T(8,128)(2,1)} async-done(((bf16[1,128,768]{2,1,0:T(8,128)(2,1)}), bf16[1,4096,768]{2,1,0:T(8,128)(2,1)}) %all-gather.10.cloned.1.call-update) | async-done | bytes 6291472 | tf_op jit(solution)/shard_map/all_gather | solution.py:157
  333.5 3.8 fusion.46
  337.2 68.2 %all-gather.12.cloned.1.call-done = bf16[1,4096,768]{2,1,0:T(8,128)(2,1)} async-done(((bf16[1,128,768]{2,1,0:T(8,128)(2,1)}), bf16[1,4096,768]{2,1,0:T(8,128)(2,1)}) %all-gather.12.cloned.1.call-update) | async-done | bytes 6291472 | tf_op jit(solution)/shard_map/all_gather | solution.py:162
  405.4 82.3 %all-gather.14.cloned.1.call-done = bf16[1,768,4096]{2,1,0:T(8,128)(2,1)} async-done(((bf16[1,768,128]{2,1,0:T(8,128)(2,1)}), bf16[1,768,4096]{2,1,0:T(8,128)(2,1)}) %all-gather.14.cloned.1.call-update) | async-done | bytes 6291472 | tf_op jit(solution)/shard_map/all_gather | solution.py:169
  487.7 7.1 %fusion.48 = bf16[128,4096]{1,0:T(8,128)(2,1)S(1)} fusion(bf16[1,768,4096]{2,1,0:T(8,128)(2,1)} %all-gather.14.cloned.1.call-done, bf16[128,4096]{1,0:T(8,128)(2,1)S(1)} %bitcast.128, bf16[1,4096,768]{2,1,0:T(8,128)(2,1)} %all-gather.12.cloned.1.call-done, f32[128,768]{1,0:T(8,128)S(1)} %fusion.46), kind=kOutput, calls=%fused_computation.65 | convolution fusion | flops 1611726848 | bytes 15073280 | tf_op jit(solution)/shard_map/dot_general | solution.py:167
  494.7 23.5 %all_to_all.10 = bf16[8,16,4096]{2,1,0:T(8,128)(2,1)S(1)} all-to-all(bf16[8,16,4096]{2,1,0:T(8,128)(2,1)S(1)} %bitcast.129), channel_id=1, replica_groups=mesh['ctx'=32,'exp'=8] {'exp'}, dimensions={0} | all-to-all | bytes 2097152 | tf_op jit(solution)/shard_map/all_to_all | solution.py:172
  (323 shorter events, 52.5 us)
Async XLA Ops:
  6.5 71.9 %all-gather.8.cloned.1.call-start = ((), (), s32[]{:S(2)}) async-start(), calls=%async_computation.3 | async-start | bytes 4325376 | tf_op jit(solution)/shard_map/all_gather | solution.py:83
  8.1 253.8 %reduce-scatter.2.cloned.1.call-start = ((), (), s32[]{:S(2)}) async-start(), calls=%async_computation.4 | async-start | bytes 2359296 | tf_op jit(solution)/shard_map/reduce_scatter | solution.py:121
  84.3 1.0 copy-start.2
  86.2 0.8 copy-start.3
  90.1 1.0 copy-start.2
  92.0 0.8 copy-start.3
  96.0 1.0 copy-start.2
  97.9 0.8 copy-start.3
  101.9 1.0 copy-start.2
  103.8 0.8 copy-start.3
  107.8 1.0 copy-start.2
  109.6 0.8 copy-start.3
  113.6 1.0 copy-start.2
  115.5 0.8 copy-start.3
  119.5 1.0 copy-start.2
  121.4 0.8 copy-start.3
  125.4 1.0 copy-start.2
  127.3 0.8 copy-start.3
  131.2 1.0 copy-start.2
  133.1 0.8 copy-start.3
  152.2 1.9 copy-start.5
  152.2 2.7 copy-start.4
  152.2 109.7 %copy-start = (bf16[32,4096]{1,0:T(8,128)(2,1)S(1)}, bf16[32,4096]{1,0:T(8,128)(2,1)}, u32[]{:S(2)}) copy-start(bf16[32,4096]{1,0:T(8,128)(2,1)} %param.21) | copy-start | bytes 786436
  152.2 181.2 %all-gather.10.cloned.1.call-start = ((), (), s32[]{:S(2)}) async-start(), calls=%async_computation.5 | async-start | bytes 6488064 | tf_op jit(solution)/shard_map/all_gather | solution.py:157
  153.0 252.4 %all-gather.12.cloned.1.call-start = ((), (), s32[]{:S(2)}) async-start(), calls=%async_computation.6 | async-start | bytes 6488064 | tf_op jit(solution)/shard_map/all_gather | solution.py:162
  153.6 334.1 %all-gather.14.cloned.1.call-start = ((), (), s32[]{:S(2)}) async-start(), calls=%async_computation.7 | async-start | bytes 6488064 | tf_op jit(solution)/shard_map/all_gather | solution.py:169
  265.5 67.9 %all-to-all-start = ((bf16[8,16,4096]{2,1,0:T(8,128)(2,1)}), bf16[8,16,4096]{2,1,0:T(8,128)(2,1)S(1)}, u32[]{:S(2)}, u32[]{:S(2)}) async-start(bf16[8,16,4096]{2,1,0:T(8,128)(2,1)} %bitcast.31), calls=%async_computation.1 | async-start | bytes 2097152 | tf_op jit(solution)/shard_map/all_to_all | solution.py:149
  494.7 23.6 %copy-start.6 = (f32[32,2]{0,1:T(2,128)S(1)}, f32[32,2]{0,1:T(2,128)}, u32[]{:S(2)}) copy-start(f32[32,2]{0,1:T(2,128)} %param.24) | copy-start | bytes 772
  494.7 23.9 %copy-start.1 = (bf16[32,4096]{1,0:T(8,128)(2,1)S(1)}, bf16[32,4096]{1,0:T(8,128)(2,1)}, u32[]{:S(2)}) copy-start(bf16[32,4096]{1,0:T(8,128)(2,1)} %reduce-scatter.2.cloned.1.call-done) | copy-start | bytes 786436
Sparse Core Ops, SparseCore 0:
  9.2 69.1 all-gather.7
  152.4 109.5 reduce-scatter.1
  263.8 69.5 all-gather.9
  335.2 70.1 all-gather.11
  407.0 80.5 all-gather.13
